TPU v7x, 256 devices: a whole 4x4x8 slice. The times are simulated.
256 devices in a mesh: gx: 32 (over y, z), gy: 8 (over x, core).
Axes of the slice: x: 4, y: 4, z: 8, core: 2. Of those that a mesh axis runs over, the one named last changes fastest.
Arguments:
- normed: bfloat16 [163840, 1024], P(('gx', 'gy')), may hold values from -6 to 6
- grad_query: bfloat16 [163840, 1024], P(('gx', 'gy')), may hold values from -0.25 to 0.25
- grad_key: bfloat16 [163840, 1024], P(('gx', 'gy')), may hold values from -0.25 to 0.25
- error: bfloat16 [512, 1024, 1024], P(('gx', 'gy')), may hold values from -8 to 8
- start_factor: float32 [2, 32, 1024], replicated, may hold values from -6 to 6
Outputs:
- new_error: bfloat16 [512, 1024, 1024], P(('gx', 'gy'))
- left_factor: float32 [2, 32, 1024], replicated
- right_factor: float32 [2, 32, 1024], replicated
All inputs are finite; a program needn't handle non-finite values.
Results may differ from a plain program's by a relative error of at most 0.001.
Values sent between devices are 32-bit elements; how exact they have to be, the bound alone decides.
A program may use at most 64 MiB of HBM per device.

v0:
```python
import jax
import jax.numpy as jnp
from jax import lax
from jax.sharding import PartitionSpec as P

HIGHEST = lax.Precision.HIGHEST
CONTRACT = (((0,), (0,)), ((), ()))


def gram_of(factor_rows):
    return jnp.einsum("bki,bli->bkl", factor_rows, factor_rows, precision=HIGHEST)


def solve_rows(gram_matrix, factor_rows):
    width = gram_matrix.shape[-1]
    identity = jnp.eye(width, dtype=jnp.float32)
    trace_value = jnp.trace(gram_matrix, axis1=1, axis2=2)
    shift_value = 1e-06 * (trace_value / width + 1.0)
    lower_factor = jnp.linalg.cholesky(gram_matrix + shift_value[:, None, None] * identity)
    return lax.linalg.triangular_solve(lower_factor, factor_rows, left_side=True, lower=True)


def local_left(merged, start_rows):
    return jnp.einsum("bkj,bij->bki", start_rows, merged, precision=HIGHEST)


def local_right(left_rows, merged):
    return jnp.einsum("bki,bij->bkj", left_rows, merged, precision=HIGHEST)


def single_factors(merged, start_rows, replicas):
    left_total = lax.psum(local_left(merged, start_rows), ("gx", "gy"))
    left_rows = solve_rows(gram_of(left_total), left_total)
    right_total = lax.psum(local_right(left_rows, merged), ("gx", "gy"))
    return (left_rows, right_total / replicas)


def on_device(normed, grad_query, grad_key, error, start_factor):
    replicas = lax.axis_size("gx") * lax.axis_size("gy")
    query_grad = lax.dot_general(normed, grad_query, CONTRACT, preferred_element_type=jnp.float32)
    query_merged = query_grad + error[0].astype(jnp.float32)
    query_left, query_right = single_factors(query_merged[None], start_factor[0:1], replicas)
    key_grad = lax.dot_general(normed, grad_key, CONTRACT, preferred_element_type=jnp.float32)
    key_merged = key_grad + error[1].astype(jnp.float32)
    key_left, key_right = single_factors(key_merged[None], start_factor[1:2], replicas)
    merged = jnp.stack([query_merged, key_merged])
    left_rows = jnp.concatenate([query_left, key_left], axis=0)
    right_rows = jnp.concatenate([query_right, key_right], axis=0)
    approx = jnp.einsum("bki,bkj->bij", left_rows, right_rows, precision=HIGHEST)
    return ((merged - approx).astype(jnp.bfloat16), left_rows, right_rows)


def solution(mesh):
    placed = (
        P(("gx", "gy"), None),
        P(("gx", "gy"), None),
        P(("gx", "gy"), None),
        P(("gx", "gy"), None, None),
        P(),
    )
    return jax.shard_map(
        on_device,
        mesh=mesh,
        in_specs=placed,
        out_specs=(P(("gx", "gy"), None, None), P(), P()),
        check_vma=False,
    )
```

profile of v0, /device:TPU:2, one launch (start us, length us, event | category | flops | bytes accessed | tf_op | source)
XLA Modules:
  0.0 575.3 jit_solution(298892361489647621)
XLA Ops:
  7.2 0.0 copy-start
  7.2 0.0 all-reduce.7.cloned.1.call-start
  7.2 1.3 copy-done
  8.5 4.0 convert_add_fusion.1
  12.5 1.8 convert_add_fusion
  14.4 0.1 copy-done.1
  14.5 4.6 convolution_bitcast_fusion.3
  19.1 4.6 convolution_bitcast_fusion.2
  23.6 0.0 all-reduce.7.cloned.1.call-update
  23.7 0.2 all-reduce.5.cloned.1.call-start
  23.9 253.5 %all-reduce.7.cloned.1.call-done = (f32[1,32,1024]{2,1,0:T(8,128)}, f32[1,32,1024]{2,1,0:T(8,128)}) async-done(((f32[1,32,1024]{2,1,0:T(8,128)}, f32[1,32,1024]{2,1,0:T(8,128)}), (f32[1,32,1024]{2,1,0:T(8,128)}, f32[1,32,1024]{2,1,0:T(8,128)})) %all-reduce.7.cloned.1.call-update) | async-done | bytes 262160 | tf_op jit(solution)/shard_map/psum | solution.py:32
  277.4 1.8 select_reduce_fusion.2
  279.9 0.1 copy.13
  280.0 2.9 custom-call.10
  282.9 0.6 compare_reduce_fusion
  283.6 0.7 fusion.14
  284.2 2.4 custom-call.11
  286.7 1.2 fusion.1
  287.9 1.8 select_reduce_fusion.3
  290.4 0.1 copy.10
  290.5 2.9 custom-call.8
  293.5 0.6 compare_reduce_fusion.1
  294.1 0.7 fusion.13
  294.8 2.4 custom-call.9
  297.2 1.4 fusion.6
  298.6 5.3 convolution_bitcast_fusion.1
  304.0 3.1 convolution_bitcast_fusion
  307.1 0.0 all-reduce.5.cloned.1.call-update
  307.2 0.0 copy-start.4
  307.2 249.5 %all-reduce.5.cloned.1.call-done = (f32[1,32,1024]{2,1,0:T(8,128)}, f32[1,32,1024]{2,1,0:T(8,128)}) async-done(((f32[1,32,1024]{2,1,0:T(8,128)}, f32[1,32,1024]{2,1,0:T(8,128)}), (f32[1,32,1024]{2,1,0:T(8,128)}, f32[1,32,1024]{2,1,0:T(8,128)})) %all-reduce.5.cloned.1.call-update) | async-done | bytes 262160 | tf_op jit(solution)/shard_map/psum | solution.py:34
  556.7 1.0 broadcast_multiply_fusion
  557.7 10.7 %fusion = bf16[2,1024,1024]{2,1,0:T(8,128)(2,1)} fusion(f32[1,1024,1024]{2,1,0:T(8,128)} %bitcast.81, f32[1,1024,1024]{2,1,0:T(8,128)} %bitcast.80, f32[2,32,1024]{2,1,0:T(8,128)S(1)} %pad_maximum_fusion, f32[2,32,1024]{2,1,0:T(8,128)S(1)} %pad_maximum_fusion.1), kind=kOutput, calls=%fused_computation.1 | convolution fusion | flops 811597824 | bytes 13107200 | tf_op jit(solution)/shard_map/bki,bkj->bij/dot_general | solution.py:49
  (22 shorter events, 0.2 us)
Async XLA Ops:
  7.2 1.3 copy-start
  7.2 5.3 copy-start.8
  7.2 270.2 %all-reduce.7.cloned.1.call-start = ((), (), s32[]{:S(2)}) async-start(), calls=%async_computation.1 | async-start | bytes 524288 | tf_op jit(solution)/shard_map/psum | solution.py:32
  8.5 4.0 copy-start.7
  12.5 2.0 copy-start.1
  12.5 2.0 copy-start.6
  14.5 4.6 copy-start.2
  23.7 533.0 %all-reduce.5.cloned.1.call-start = ((), (), s32[]{:S(2)}) async-start(), calls=%async_computation | async-start | bytes 524288 | tf_op jit(solution)/shard_map/psum | solution.py:34
  297.2 6.7 %copy-start.3 = (f32[1024,1024]{1,0:T(8,128)S(1)}, f32[1024,1024]{1,0:T(8,128)}, u32[]{:S(2)}) copy-start(f32[1024,1024]{1,0:T(8,128)} %copy-done.2) | copy-start | bytes 12582916
  307.2 261.3 %copy-start.4 = (f32[2,32,1024]{2,1,0:T(8,128)}, f32[2,32,1024]{2,1,0:T(8,128)S(1)}, u32[]{:S(2)}) copy-start(f32[2,32,1024]{2,1,0:T(8,128)S(1)} %pad_maximum_fusion) | copy-start | bytes 786436
  557.7 10.7 %copy-start.5 = (f32[2,32,1024]{2,1,0:T(8,128)}, f32[2,32,1024]{2,1,0:T(8,128)S(1)}, u32[]{:S(2)}) copy-start(f32[2,32,1024]{2,1,0:T(8,128)S(1)} %pad_maximum_fusion.1) | copy-start | bytes 786436
Sparse Core Ops, SparseCore 0:
  23.8 253.5 all-reduce.6
  307.2 249.3 all-reduce.4
where the time goes:
time: 576 us; the launch traced here: 575 us
  waiting for transfers between devices  503 us (87%)
  matrix products  40.5 us (7%)
  between operations  15.5 us (3%)
  other arithmetic  14.4 us (2%)
    psum x1, waiting for transfers between devices, single_factors(): left_total = lax.psum(local_left(merged, start_rows), ('gx', 'gy'))  254 us
    psum x1, waiting for transfers between devices, single_factors(): right_total = lax.psum(local_right(left_rows, merged), ('gx', 'gy'))  250 us
  transfers between devices with their start and end apart: 2, of which 2 were waited for; matrix products, arithmetic and copies ran while one was open for 0% of the time, Pallas kernels for 0%

commit v1 on v0

--- a/solution.py
+++ b/solution.py
@@ -29,7 +29,7 @@
 
 
 def single_factors(merged, start_rows, replicas):
-    left_total = lax.psum(local_left(merged, start_rows), ("gx", "gy"))
+    left_total = lax.psum(lax.psum(local_left(merged, start_rows), "gy"), "gx")
     left_rows = solve_rows(gram_of(left_total), left_total)
     right_total = lax.psum(local_right(left_rows, merged), ("gx", "gy"))
     return (left_rows, right_total / replicas)

time: 576 us -> 535 us (0.929)
  waiting for transfers between devices: 503 us -> 463 us
    psum x1 -> x2, waiting for transfers between devices: 254 us -> 215 us  [single_factors(): left_total = lax.psum(lax.psum(local_left(merged, start_rows), 'gy'), 'gx')]
  transfers between devices with their start and end apart: 2 -> 3, of which waited for: 2 -> 3; matrix products, arithmetic and copies ran while one was open for 0% -> 0% of each run, Pallas kernels for 0% -> 0%
where the time goes in v1:
time: 535 us
  waiting for transfers between devices  463 us (87%)
  matrix products  40.5 us (8%)
  between operations  15.2 us (3%)
  other arithmetic  14.4 us (3%)
    psum x1, waiting for transfers between devices, single_factors(): right_total = lax.psum(local_right(left_rows, merged), ('gx', 'gy'))  248 us
    psum x2, waiting for transfers between devices, single_factors(): left_total = lax.psum(lax.psum(local_left(merged, start_rows), 'gy'), 'gx')  215 us
    dot_general x1, matrix products, on_device(): jnp.einsum('bki,bkj->bij', left_rows, right_rows, precision=HIGHEST)  10.7 us
  transfers between devices with their start and end apart: 3, of which 3 were waited for; matrix products, arithmetic and copies ran while one was open for 0% of the time, Pallas kernels for 0%

profile of v1, /device:TPU:2, one launch (start us, length us, event | category | flops | bytes accessed | tf_op | source)
XLA Modules:
  0.0 535.2 jit_solution(12552644678493231196)
XLA Ops:
  7.2 0.0 all-reduce.11.cloned.1.call-start
  7.2 1.3 copy-done
  8.5 4.0 convert_add_fusion.1
  12.5 1.8 convert_add_fusion
  14.4 0.1 copy-done.1
  14.5 4.6 convolution_bitcast_fusion.3
  19.1 4.6 convolution_bitcast_fusion.2
  23.7 0.0 all-reduce.9.cloned.1.call-start
  23.7 65.9 %all-reduce.11.cloned.1.call-done = (f32[1,32,1024]{2,1,0:T(8,128)}, f32[1,32,1024]{2,1,0:T(8,128)}) async-done(((f32[1,32,1024]{2,1,0:T(8,128)}, f32[1,32,1024]{2,1,0:T(8,128)}), (f32[1,32,1024]{2,1,0:T(8,128)}, f32[1,32,1024]{2,1,0:T(8,128)})) %all-reduce.11.cloned.1.call-update) | async-done | bytes 262160 | tf_op jit(solution)/shard_map/psum | solution.py:32
  89.6 0.0 all-reduce.9.cloned.1.call-update
  89.7 0.2 all-reduce.7.cloned.1.call-start
  89.9 149.3 %all-reduce.9.cloned.1.call-done = (f32[1,32,1024]{2,1,0:T(8,128)}, f32[1,32,1024]{2,1,0:T(8,128)}) async-done(((f32[1,32,1024]{2,1,0:T(8,128)}, f32[1,32,1024]{2,1,0:T(8,128)}), (f32[1,32,1024]{2,1,0:T(8,128)}, f32[1,32,1024]{2,1,0:T(8,128)})) %all-reduce.9.cloned.1.call-update) | async-done | bytes 262160 | tf_op jit(solution)/shard_map/psum | solution.py:32
  239.2 1.8 select_reduce_fusion.2
  241.7 0.1 copy.13
  241.8 2.9 custom-call.10
  244.7 0.6 compare_reduce_fusion
  245.3 0.7 fusion.14
  246.0 2.4 custom-call.11
  248.4 1.2 fusion.1
  249.7 1.8 select_reduce_fusion.3
  252.2 0.1 copy.10
  252.3 2.9 custom-call.8
  255.2 0.6 compare_reduce_fusion.1
  255.9 0.7 fusion.13
  256.5 2.4 custom-call.9
  259.0 1.4 fusion.6
  260.4 5.3 convolution_bitcast_fusion.1
  265.7 3.1 convolution_bitcast_fusion
  268.9 0.0 all-reduce.7.cloned.1.call-update
  268.9 248.0 %all-reduce.7.cloned.1.call-done = (f32[1,32,1024]{2,1,0:T(8,128)}, f32[1,32,1024]{2,1,0:T(8,128)}) async-done(((f32[1,32,1024]{2,1,0:T(8,128)}, f32[1,32,1024]{2,1,0:T(8,128)}), (f32[1,32,1024]{2,1,0:T(8,128)}, f32[1,32,1024]{2,1,0:T(8,128)})) %all-reduce.7.cloned.1.call-update) | async-done | bytes 262160 | tf_op jit(solution)/shard_map/psum | solution.py:34
  516.9 1.0 broadcast_multiply_fusion
  517.9 10.7 %fusion = bf16[2,1024,1024]{2,1,0:T(8,128)(2,1)} fusion(f32[1,1024,1024]{2,1,0:T(8,128)} %bitcast.81, f32[1,1024,1024]{2,1,0:T(8,128)} %bitcast.80, f32[2,32,1024]{2,1,0:T(8,128)S(1)} %pad_maximum_fusion, f32[2,32,1024]{2,1,0:T(8,128)S(1)} %pad_maximum_fusion.1), kind=kOutput, calls=%fused_computation.1 | convolution fusion | flops 811597824 | bytes 13107200 | tf_op jit(solution)/shard_map/bki,bkj->bij/dot_general | solution.py:49
  (25 shorter events, 0.2 us)
Async XLA Ops:
  7.2 1.3 copy-start
  7.2 5.3 copy-start.8
  7.2 82.5 %all-reduce.11.cloned.1.call-start = ((), (), s32[]{:S(2)}) async-start(), calls=%async_computation.2 | async-start | bytes 524288 | tf_op jit(solution)/shard_map/psum | solution.py:32
  8.5 4.0 copy-start.7
  12.5 2.0 copy-start.1
  12.5 2.0 copy-start.6
  14.5 4.6 copy-start.2
  23.7 215.5 %all-reduce.9.cloned.1.call-start = ((), (), s32[]{:S(2)}) async-start(), calls=%async_computation.1 | async-start | bytes 524288 | tf_op jit(solution)/shard_map/psum | solution.py:32
  89.7 427.2 %all-reduce.7.cloned.1.call-start = ((), (), s32[]{:S(2)}) async-start(), calls=%async_computation | async-start | bytes 524288 | tf_op jit(solution)/shard_map/psum | solution.py:34
  259.0 6.7 %copy-start.3 = (f32[1024,1024]{1,0:T(8,128)S(1)}, f32[1024,1024]{1,0:T(8,128)}, u32[]{:S(2)}) copy-start(f32[1024,1024]{1,0:T(8,128)} %copy-done.2) | copy-start | bytes 12582916
  268.9 259.7 %copy-start.4 = (f32[2,32,1024]{2,1,0:T(8,128)}, f32[2,32,1024]{2,1,0:T(8,128)S(1)}, u32[]{:S(2)}) copy-start(f32[2,32,1024]{2,1,0:T(8,128)S(1)} %pad_maximum_fusion) | copy-start | bytes 786436
  517.9 10.7 %copy-start.5 = (f32[2,32,1024]{2,1,0:T(8,128)}, f32[2,32,1024]{2,1,0:T(8,128)S(1)}, u32[]{:S(2)}) copy-start(f32[2,32,1024]{2,1,0:T(8,128)S(1)} %pad_maximum_fusion.1) | copy-start | bytes 786436
Sparse Core Ops, SparseCore 0:
  23.8 65.8 all-reduce.10
  93.6 145.5 all-reduce.8
  269.0 247.8 all-reduce.6
